TPU v7x, 32 devices: a whole 2x2x4 slice. The times are simulated.
32 devices in a mesh: section: 2 (over core), rep: 2 (over x), tp: 8 (over z, y).
Axes of the slice: x: 2, y: 2, z: 4, core: 2. Of those that a mesh axis runs over, the one named last changes fastest.
Arguments:
- states: bfloat16 [2, 2, 256, 8192], P('section', 'rep', None, 'tp'), may hold values from -6 to 6
- q_weight: bfloat16 [8192, 4096], P(None, 'tp'), may hold values from -0.0625 to 0.0625
- kv_weight: bfloat16 [8192, 1024], P('tp'), may hold values from -0.0625 to 0.0625
- o_weight: bfloat16 [4096, 8192], P(None, 'tp'), may hold values from -0.09375 to 0.09375
- store_keys: bfloat16 [2, 2, 4096, 512], P('section', 'rep', 'tp'), may hold values from -170 to 170
- store_values: bfloat16 [2, 2, 4096, 512], P('section', 'rep', 'tp'), may hold values from -48 to 48
- prefix_len: int32 [2], replicated, may hold values from 1024 to 4096
- cache_len: int32 [2, 4], P('rep'), may hold values from 128 to 1024
- parents: int32 [2, 4, 64], P('rep'), may hold values from -1 to 62, as said below
Outputs:
- attn_out: bfloat16 [2, 2, 256, 8192], P('section', 'rep', None, 'tp')
Inputs may be any that keep to these rules, and one draw needn't show every extreme that they name: `parents`: each node's parent is an earlier node of the same tree; only node 0 has -1.
All inputs are finite; a program needn't handle non-finite values.
Results may differ from a plain program's by a relative error of at most 0.0065.
The roundings to bfloat16 on the way count: a program that leaves them out, or rounds other values in their place, can miss the bound.
Values may be sent and summed in bfloat16 or wider, within the bound.
No kernel may reach another device: no remote copies, remote signals or barrier semaphores. Data moves between devices by JAX's collectives and lax.ppermute only.
A program may use at most 128 MiB of HBM per device.

v0:
```python
import jax
import jax.numpy as jnp
from jax import lax
from jax.sharding import PartitionSpec as P

HD = 128
SEQS = 4
NODES = 64
CACHE = 1024
ROPE_BASE = 500000.0
MASKED_SCORE = -1e30


def passed_along(block, axis, distance):
    devices = range(lax.axis_size(axis))
    route = [(i - distance, i) for i in devices if i - distance in devices]
    return lax.ppermute(block, axis, route)


def rotate(vectors, positions):
    head_size = vectors.shape[-1]
    half_width = head_size // 2
    exponent = jnp.arange(half_width, dtype=jnp.float32) * (-2.0 / head_size)
    frequency = jnp.exp(exponent * jnp.log(jnp.float32(ROPE_BASE)))
    angles = positions.astype(jnp.float32)[:, None] * frequency[None, :]
    cosine = jnp.cos(angles)[:, None, :]
    sine_of = jnp.sin(angles)[:, None, :]
    front_half = vectors[..., :half_width]
    back_half = vectors[..., half_width:]
    return jnp.concatenate(
        [front_half * cosine - back_half * sine_of, back_half * cosine + front_half * sine_of],
        axis=-1,
    )


def closure(parents):
    node_count = parents.shape[-1]
    node_ids = jnp.arange(node_count, dtype=jnp.int32)
    reached = (parents[:, :, None] == node_ids[None, None, :]).astype(jnp.float32)
    reached = reached + jnp.eye(node_count, dtype=jnp.float32)[None]
    for level_index in range(max(1, (node_count - 1).bit_length())):
        reached = jnp.minimum(
            jnp.einsum("sij,sjk->sik", reached, reached, precision=lax.Precision.HIGHEST), 1.0
        )
    return reached


def partial_attend(queries, all_keys, all_values, visible):
    row_count = queries.shape[0]
    kv_heads = all_keys.shape[1] // HD
    group_size = queries.shape[1] // all_keys.shape[1]
    row_tops = []
    row_totals = []
    mixtures = []
    for kv_head in range(kv_heads):
        query_block = queries[
            :, kv_head * group_size * HD : (kv_head + 1) * group_size * HD
        ].reshape(row_count * group_size, HD)
        key_block = all_keys[:, kv_head * HD : (kv_head + 1) * HD]
        value_block = all_values[:, kv_head * HD : (kv_head + 1) * HD]
        scores = lax.dot_general(
            query_block, key_block, (((1,), (1,)), ((), ())), preferred_element_type=jnp.float32
        )
        scores = scores.reshape(row_count, group_size, -1) * HD ** (-0.5)
        scores = jnp.where(visible[:, None, :], scores, MASKED_SCORE)
        row_top = jnp.max(scores, axis=-1)
        weights = jnp.where(visible[:, None, :], jnp.exp(scores - row_top[..., None]), 0.0)
        row_total = jnp.sum(weights, axis=-1)
        mixed_rows = jnp.dot(
            weights.astype(jnp.bfloat16).reshape(row_count * group_size, -1),
            value_block,
            preferred_element_type=jnp.float32,
        )
        mixed_rows = (
            mixed_rows.reshape(row_count, group_size, HD) / jnp.maximum(row_total, 1.0)[..., None]
        )
        row_tops.append(row_top)
        row_totals.append(row_total)
        mixtures.append(mixed_rows.reshape(row_count, group_size * HD).astype(jnp.bfloat16))
    return (
        jnp.concatenate(row_tops, axis=1),
        jnp.concatenate(row_totals, axis=1),
        jnp.concatenate(mixtures, axis=1),
    )


def finish(tops, totals, parts):
    piece_count, row_count, head_count = tops.shape
    best = jnp.max(tops, axis=0)
    factor = jnp.exp(tops - best[None]) * totals
    denominator = jnp.sum(factor, axis=0)
    numerator = jnp.sum(
        parts.astype(jnp.float32).reshape(piece_count, row_count, head_count, HD)
        * factor[..., None],
        axis=0,
    )
    return (
        (numerator / denominator[..., None])
        .reshape(row_count, head_count * HD)
        .astype(jnp.bfloat16)
    )


def per_device(
    states, q_weight, kv_weight, o_weight, store_keys, store_values, prefix_len, cache_len, parents
):
    inputs = states[0, 0]
    row_count = inputs.shape[0]
    tp_count = lax.axis_size("tp")
    tp_index = lax.axis_index("tp")
    replica = lax.axis_index("rep")
    rep_count = lax.axis_size("rep")
    decoding = lax.axis_index("section") == 1
    own_cols = q_weight.shape[1]
    kv_width = kv_weight.shape[1] // 2
    block_rows = row_count // tp_count
    first_row = tp_index * block_rows
    row_ids = jnp.arange(row_count, dtype=jnp.int32)
    seq_of = row_ids // NODES
    own_prefix = prefix_len[replica]
    reached = closure(parents[0])
    depths = (jnp.sum(reached, axis=-1).astype(jnp.int32) - 1).reshape(row_count)
    seq_lengths = jnp.broadcast_to(cache_len[0][:, None], (SEQS, NODES)).reshape(row_count)
    tree_base = jnp.where(seq_of == 0, own_prefix + row_count, seq_lengths)
    positions = jnp.where(decoding, tree_base + depths, own_prefix + row_ids)
    query_sums = jnp.dot(
        lax.all_gather(inputs, "tp", axis=1, tiled=True),
        q_weight,
        preferred_element_type=jnp.float32,
    )
    own_queries = (
        rotate(query_sums.reshape(row_count, own_cols // HD, HD), positions)
        .reshape(row_count, own_cols)
        .astype(jnp.bfloat16)
    )
    queries = lax.all_gather(own_queries, "tp", axis=1, tiled=True)
    kv_rows = lax.psum_scatter(
        jnp.dot(inputs, kv_weight, preferred_element_type=jnp.float32).astype(jnp.bfloat16),
        "tp",
        scatter_dimension=0,
        tiled=True,
    ).astype(jnp.float32)
    local_pos = lax.dynamic_slice_in_dim(positions, first_row, block_rows, 0)
    new_keys = (
        rotate(kv_rows[:, :kv_width].reshape(block_rows, -1, HD), local_pos)
        .reshape(block_rows, kv_width)
        .astype(jnp.bfloat16)
    )
    new_values = kv_rows[:, kv_width:].astype(jnp.bfloat16)
    moved = passed_along(jnp.stack([new_keys, new_values]), ("section", "rep"), rep_count)
    tail_keys = moved[0]
    tail_values = moved[1]
    store_rows = store_keys.shape[2]
    store_pos = tp_index * store_rows + jnp.arange(store_rows, dtype=jnp.int32)
    prefill_store = jnp.broadcast_to(store_pos[None, :] < own_prefix, (row_count, store_rows))
    decode_store = (store_pos[None, :] // CACHE == seq_of[:, None]) & (
        store_pos[None, :] % CACHE < seq_lengths[:, None]
    )
    block_ids = first_row + jnp.arange(block_rows, dtype=jnp.int32)
    prefill_new = block_ids[None, :] <= row_ids[:, None]
    eye_seq = (jnp.arange(SEQS)[:, None] == jnp.arange(SEQS)[None, :]).astype(jnp.float32)
    tree_full = (eye_seq[:, None, :, None] * reached[:, :, None, :]).reshape(row_count, row_count)
    decode_new = lax.dynamic_slice_in_dim(tree_full, first_row, block_rows, 1) > 0.5
    tail_seen = jnp.broadcast_to((seq_of == 0)[:, None], (row_count, block_rows))
    decode_mask = jnp.concatenate([decode_store, decode_new, tail_seen], axis=1)
    prefill_mask = jnp.concatenate([prefill_store, prefill_new, jnp.zeros_like(tail_seen)], axis=1)
    visible = jnp.where(decoding, decode_mask, prefill_mask)
    all_keys = jnp.concatenate([store_keys[0, 0], new_keys, tail_keys], axis=0)
    all_values = jnp.concatenate([store_values[0, 0], new_values, tail_values], axis=0)
    row_tops, row_totals, mixtures = partial_attend(queries, all_keys, all_values, visible)
    peer_tops, peer_totals, peer_mix = (
        lax.all_to_all(row_tops[None], "tp", split_axis=1, concat_axis=0, tiled=True),
        lax.all_to_all(row_totals[None], "tp", split_axis=1, concat_axis=0, tiled=True),
        lax.all_to_all(
            mixtures[None].astype(jnp.float32), "tp", split_axis=1, concat_axis=0, tiled=True
        ).astype(jnp.bfloat16),
    )
    own_rows = finish(peer_tops, peer_totals, peer_mix)
    result = jnp.dot(
        lax.all_gather(own_rows, "tp", axis=0, tiled=True),
        o_weight,
        preferred_element_type=jnp.float32,
    )
    return result.astype(jnp.bfloat16)[None, None]


def solution(mesh):
    in_specs = (
        P("section", "rep", None, "tp"),
        P(None, "tp"),
        P("tp", None),
        P(None, "tp"),
        P("section", "rep", "tp", None),
        P("section", "rep", "tp", None),
        P(),
        P("rep", None),
        P("rep", None, None),
    )
    out_specs = P("section", "rep", None, "tp")
    return jax.shard_map(
        per_device, mesh=mesh, in_specs=in_specs, out_specs=out_specs, check_vma=False
    )
```

profile of v0, /device:TPU:0, one launch (start us, length us, event | category | flops | bytes accessed | tf_op | source)
XLA Modules:
  0.0 400.3 jit_solution(13573577960373049642)
XLA Ops:
  6.5 0.7 all-gather.9.cloned.1.call-update
  7.3 0.8 copy-done
  8.1 2.5 convolution_convert_fusion.1
  10.8 1.1 convolution_minimum_fusion.5
  11.9 0.3 convolution_minimum_fusion.4
  12.2 0.3 convolution_minimum_fusion.3
  12.4 0.3 convolution_minimum_fusion.2
  12.7 0.3 convolution_minimum_fusion.1
  13.0 0.4 fusion.66
  13.6 0.6 dynamic_slice.10
  14.8 0.6 fusion.63
  15.4 0.5 multiply_cosine_fusion
  16.0 69.1 %all-gather.9.cloned.1.call-done = bf16[1,1,256,8192]{3,2,1,0:T(8,128)(2,1)} async-done(((bf16[1,1,256,1024]{3,2,1,0:T(8,128)(2,1)}), bf16[1,1,256,8192]{3,2,1,0:T(8,128)(2,1)}) %all-gather.9.cloned.1.call-update) | async-done | bytes 4194320 | tf_op jit(solution)/shard_map/all_gather | solution.py:127
  85.1 7.0 %fusion = f32[256,512]{1,0:T(8,128)S(1)} fusion(bf16[8192,512]{1,0:T(8,128)(2,1)} %param.10, bf16[1,1,256,8192]{3,2,1,0:T(8,128)(2,1)} %all-gather.9.cloned.1.call-done), kind=kOutput, calls=%fused_computation.9 | convolution fusion | flops 2147483648 | bytes 13107200 | tf_op jit(solution)/shard_map/dot_general | solution.py:126
  92.2 0.5 subtract_convert_fusion
  92.7 0.4 pad_maximum_fusion.2
  93.1 0.9 copy.50
  94.3 0.3 mul.173
  94.6 0.6 fusion.45
  95.9 54.1 %reduce-scatter.2.cloned.1.call-done = bf16[32,1024]{1,0:T(8,128)(2,1)} async-done(((bf16[256,1024]{1,0:T(8,128)(2,1)}), bf16[32,1024]{1,0:T(8,128)(2,1)}) %reduce-scatter.2.cloned.1.call-update) | async-done | bytes 65552 | tf_op jit(solution)/shard_map/reduce_scatter | solution.py:137
  150.0 0.8 fusion.65
  151.1 1.3 collective-permute-start
  152.4 0.2 add_select_fusion
  152.7 0.6 collective-permute-done
  153.3 1.3 pad_maximum_fusion
  154.6 45.7 %all-gather.5.cloned.1.call-done = bf16[256,4096]{0,1:T(8,128)(2,1)} async-done(((bf16[256,512]{0,1:T(8,128)(2,1)}), bf16[256,4096]{0,1:T(8,128)(2,1)}) %all-gather.5.cloned.1.call-update) | async-done | bytes 2097168 | tf_op jit(solution)/shard_map/all_gather | solution.py:136
  200.3 1.7 fusion.64
  201.9 0.8 fusion.37
  202.7 0.8 fusion.36
  203.5 0.9 fusion.2
  204.3 0.5 copy-done.3
  204.8 4.7 %fusion.6 = (f32[256,8]{0,1:T(8,128)S(1)}, f32[256,8]{0,1:T(8,128)S(1)}, f32[256,8]{0,1:T(8,128)S(1)}, f32[256,8]{0,1:T(8,128)S(1)}, f32[256,8,576]{0,2,1:T(8,128)}) fusion(f32[256,8,576]{0,2,1:T(8,128)S(1)} %get-tuple-element.36, f32[256,8]{0,1:T(8,128)S(1)} %get-tuple-element.35, pred[256,576]{0,1:T(8,128)(4,1)S(1)} %add_select_fusion, ...), kind=kOutput, calls=%fused_computation.17 | convolution fusion | flops 318496768 | bytes 19734528 | tf_op jit(solution)/shard_map/dot_general | solution.py:61
  209.6 0.5 broadcast.416
  210.1 1.0 reduce.5
  211.1 0.7 reshape.512
  211.9 3.5 all-to-all-start.1
  215.4 7.0 %fusion.8 = (f32[256,8]{0,1:T(8,128)S(1)}, f32[256,8]{0,1:T(8,128)S(1)}, f32[256,8]{0,1:T(8,128)S(1)}) fusion(f32[256,8,576]{0,2,1:T(8,128)} %get-tuple-element.37, f32[256,8]{0,1:T(8,128)S(1)} %get-tuple-element.6, pred[256,576]{0,1:T(8,128)(4,1)S(1)} %add_select_fusion, f32[256,8]{0,1:T(8,128)S(1)} %get-tuple-element.7, f32[256,8,576]{0,2,1:T(8,128)} %copy-done.3, ...), kind=kLoop, calls=%fused_computation.19 | loop fusion | flops 17688576 | bytes 14352384 | tf_op jit(solution)/shard_map/reduce_sum | solution.py:68
  222.4 3.8 divide_convert_fusion.3
  226.2 2.1 divide_convert_fusion.2
  228.3 2.1 divide_convert_fusion.1
  230.4 2.1 divide_convert_fusion
  232.6 1.0 reduce.3
  233.6 0.7 reshape.510
  234.3 1.0 copy.55
  235.3 1.0 copy.56
  236.4 2.5 copy.57
  238.8 3.6 copy.58
  242.5 5.7 %all-to-all-start.2 = ((f32[8,1,1024]{2,1,0:T(1,128)}), f32[8,1,1024]{2,1,0:T(1,128)S(1)}, u32[]{:S(2)}, u32[]{:S(2)}) async-start(f32[8,1,1024]{2,1,0:T(1,128)} %reshape.510), calls=%async_computation.3 | async-start | bytes 65536 | tf_op jit(solution)/shard_map/all_to_all | solution.py:173
  248.2 6.6 %fusion.67 = bf16[256,1,4096]{2,1,0:T(2,128)(2,1)} fusion(bf16[1,256,1024]{2,0,1:T(2,128)(2,1)} %copy.58, bf16[1,256,1024]{2,0,1:T(2,128)(2,1)S(1)} %copy.57, bf16[1,256,1024]{2,0,1:T(2,128)(2,1)S(1)} %copy.56, bf16[1,256,1024]{2,0,1:T(2,128)(2,1)S(1)} %copy.55), kind=kLoop, calls=%fused_computation.139 | loop fusion | flops 8388608 | bytes 4194304
  254.8 0.5 broadcast.415
  255.3 13.5 %reduce.2 = bf16[256,4096]{1,0:T(8,128)(2,1)S(1)} reduce(bf16[256,1,4096]{2,1,0:T(2,128)(2,1)} %fusion.67, bf16[]{:T(256)} %broadcast.415), dimensions={1}, to_apply=%fusion.67.reduce_sub_computation | reduce | bytes 4194306
  268.8 3.8 reshape.508
  272.6 6.0 %all-to-all-start = ((bf16[8,2,65536]{2,1,0:T(2,128)(2,1)}), bf16[8,2,65536]{2,1,0:T(2,128)(2,1)S(1)}, u32[]{:S(2)}, u32[]{:S(2)}) async-start(bf16[8,2,65536]{2,1,0:T(2,128)(2,1)} %reshape.508), calls=%async_computation.1 | async-start | bytes 4194304 | tf_op jit(solution)/shard_map/all_to_all | solution.py:174
  278.6 0.3 all-gather.7.cloned.1.call-start
  278.8 0.7 reduce.6
  279.8 0.7 reduce.4
  280.5 0.2 reshape.511
  280.8 44.4 %all-to-all-done = bf16[8,2,65536]{2,1,0:T(2,128)(2,1)S(1)} async-done(((bf16[8,2,65536]{2,1,0:T(2,128)(2,1)}), bf16[8,2,65536]{2,1,0:T(2,128)(2,1)S(1)}, u32[]{:S(2)}, u32[]{:S(2)}) %all-to-all-start) | async-done | bytes 2097184 | tf_op jit(solution)/shard_map/all_to_all | solution.py:174
  325.2 4.3 %reshape.509 = bf16[256,1,4096]{2,1,0:T(2,128)(2,1)} reshape(bf16[8,2,65536]{2,1,0:T(2,128)(2,1)S(1)} %all-to-all-done) | data formatting | bytes 4194304
  329.5 6.5 %bitcast_convert_fusion = f32[1,256,4096]{2,0,1:T(1,128)S(1)} fusion(bf16[256,1,4096]{2,1,0:T(2,128)(2,1)} %reshape.509), kind=kLoop, calls=%fused_computation.138 | loop fusion | flops 1048576 | bytes 6291456 | tf_op jit(solution)/shard_map/convert_element_type | solution.py:93
  336.0 1.4 multiply_reduce_fusion
  337.6 0.8 copy.74
  338.5 48.1 %all-gather.7.cloned.1.call-done = bf16[256,4096]{1,0:T(8,128)(2,1)} async-done(((bf16[32,4096]{1,0:T(8,128)(2,1)}), bf16[256,4096]{1,0:T(8,128)(2,1)}) %all-gather.7.cloned.1.call-update) | async-done | bytes 2097168 | tf_op jit(solution)/shard_map/all_gather | solution.py:180
  386.5 7.3 %fusion.26 = bf16[1,1,256,1024]{3,2,1,0:T(8,128)(2,1)} fusion(bf16[256,4096]{1,0:T(8,128)(2,1)} %all-gather.7.cloned.1.call-done, bf16[4096,1024]{1,0:T(8,128)(2,1)} %param.12), kind=kOutput, calls=%fused_computation.35 | convolution fusion | flops 2147745792 | bytes 11010048 | tf_op jit(solution)/shard_map/dot_general | solution.py:179
  (78 shorter events, 2.5 us)
Async XLA Ops:
  6.5 1.6 copy-start
  6.5 6.9 %copy-start.6 = (s32[1,4]{1,0:T(1,128)S(1)}, s32[1,4]{1,0:T(1,128)}, u32[]{:S(2)}) copy-start(s32[1,4]{1,0:T(1,128)} %param.16) | copy-start | bytes 52
  6.5 7.0 %copy-start.7 = (s32[2]{0:T(128)S(1)}, s32[2]{0:T(128)}, u32[]{:S(2)}) copy-start(s32[2]{0:T(128)} %param.15) | copy-start | bytes 28
  6.5 78.5 %all-gather.9.cloned.1.call-start = ((), (), s32[]{:S(2)}) async-start(), calls=%async_computation.7 | async-start | bytes 4718592 | tf_op jit(solution)/shard_map/all_gather | solution.py:127
  7.3 142.8 %reduce-scatter.2.cloned.1.call-start = ((), (), s32[]{:S(2)}) async-start(), calls=%async_computation.5 | async-start | bytes 589824 | tf_op jit(solution)/shard_map/reduce_scatter | solution.py:137
  10.7 189.6 %all-gather.5.cloned.1.call-start = ((), (), s32[]{:S(2)}) async-start(), calls=%async_computation.4 | async-start | bytes 2359296 | tf_op jit(solution)/shard_map/all_gather | solution.py:136
  151.1 2.2 collective-permute-start
  202.7 2.2 copy-start.3
  203.4 6.0 %copy-start.2 = (f32[256,8,576]{0,2,1:T(8,128)}, f32[256,8,576]{0,2,1:T(8,128)S(1)}, u32[]{:S(2)}) copy-start(f32[256,8,576]{0,2,1:T(8,128)S(1)} %fusion.36) | copy-start | bytes 14155780
  204.3 5.2 %copy-start.4 = (f32[256,8,576]{0,2,1:T(8,128)}, f32[256,8,576]{0,2,1:T(8,128)S(1)}, u32[]{:S(2)}) copy-start(f32[256,8,576]{0,2,1:T(8,128)S(1)} %get-tuple-element.36) | copy-start | bytes 14155780
  210.1 16.1 %slice-start.4 = ((s8[4718592]{0:T(1024)(128)(4,1)}), s8[524288]{0:T(1024)(128)(4,1)S(1)}, s32[]{:S(2)}) async-start(s8[4718592]{0:T(1024)(128)(4,1)} %bitcast.102), calls=%async_computation.12 | async-start | bytes 1048576
  211.9 30.6 %all-to-all-start.1 = ((f32[8,1,1024]{2,1,0:T(1,128)}), f32[8,1,1024]{2,1,0:T(1,128)S(1)}, u32[]{:S(2)}, u32[]{:S(2)}) async-start(f32[8,1,1024]{2,1,0:T(1,128)} %reshape.512), calls=%async_computation.2 | async-start | bytes 65536 | tf_op jit(solution)/shard_map/all_to_all | solution.py:172
  215.4 10.8 %slice-start.5 = ((s8[4718592]{0:T(1024)(128)(4,1)}), s8[4194304]{0:T(1024)(128)(4,1)S(1)}, s32[]{:S(2)}) async-start(s8[4718592]{0:T(1024)(128)(4,1)} %bitcast.102), calls=%async_computation.13 | async-start | bytes 8388608
  222.4 5.9 %slice-start.2 = ((s8[4718592]{0:T(1024)(128)(4,1)}), s8[4194304]{0:T(1024)(128)(4,1)S(1)}, s32[]{:S(2)}) async-start(s8[4718592]{0:T(1024)(128)(4,1)} %bitcast.99), calls=%async_computation.10 | async-start | bytes 8388608
  226.2 2.1 slice-start.3
  226.2 4.2 %slice-start = ((s8[4718592]{0:T(1024)(128)(4,1)}), s8[4194304]{0:T(1024)(128)(4,1)S(1)}, s32[]{:S(2)}) async-start(s8[4718592]{0:T(1024)(128)(4,1)} %bitcast.97), calls=%async_computation.8 | async-start | bytes 8388608
  228.3 2.1 slice-start.1
  230.4 4.9 %copy-start.5 = (bf16[256,8,128]{0,2,1:T(8,128)(2,1)S(1)}, bf16[256,8,128]{0,2,1:T(8,128)(2,1)}, u32[]{:S(2)}) copy-start(bf16[256,8,128]{0,2,1:T(8,128)(2,1)} %divide_convert_fusion.2) | copy-start | bytes 1572868
  242.5 30.1 %all-to-all-start.2 = ((f32[8,1,1024]{2,1,0:T(1,128)}), f32[8,1,1024]{2,1,0:T(1,128)S(1)}, u32[]{:S(2)}, u32[]{:S(2)}) async-start(f32[8,1,1024]{2,1,0:T(1,128)} %reshape.510), calls=%async_computation.3 | async-start | bytes 65536 | tf_op jit(solution)/shard_map/all_to_all | solution.py:173
  272.6 52.6 %all-to-all-start = ((bf16[8,2,65536]{2,1,0:T(2,128)(2,1)}), bf16[8,2,65536]{2,1,0:T(2,128)(2,1)S(1)}, u32[]{:S(2)}, u32[]{:S(2)}) async-start(bf16[8,2,65536]{2,1,0:T(2,128)(2,1)} %reshape.508), calls=%async_computation.1 | async-start | bytes 4194304 | tf_op jit(solution)/shard_map/all_to_all | solution.py:174
  278.6 108.0 %all-gather.7.cloned.1.call-start = ((), (), s32[]{:S(2)}) async-start(), calls=%async_computation.6 | async-start | bytes 2359296 | tf_op jit(solution)/shard_map/all_gather | solution.py:180
  386.5 7.3 %copy-start.1 = (bf16[1024,1024]{1,0:T(8,128)(2,1)S(1)}, bf16[1024,1024]{1,0:T(8,128)(2,1)}, u32[]{:S(2)}) copy-start(bf16[1024,1024]{1,0:T(8,128)(2,1)} %param.11) | copy-start | bytes 6291460
Sparse Core Ops, SparseCore 0:
  9.5 75.4 all-gather.8
  88.4 61.5 reduce-scatter.1
  152.2 48.0 all-gather.4
  338.6 47.8 all-gather.6
where the time goes:
time: 401 us; the launch traced here: 400 us
  waiting for transfers between devices  263 us (66%)
  other arithmetic  44.4 us (11%)
  matrix products  36.4 us (9%)
  local copies, waits for them, and re-layouts  25.7 us (6%)
  starting transfers between devices  16.9 us (4%)
  between operations  14.3 us (4%)
    all_gather x1, waiting for transfers between devices, per_device(): lax.all_gather(inputs, 'tp', axis=1, tiled=True)  69.1 us
    reduce_scatter x1, waiting for transfers between devices, per_device(): lax.psum_scatter(jnp.dot(inputs, kv_weight, preferred_element_type=jnp.fl...  54.1 us
    all_gather x1, waiting for transfers between devices, per_device(): lax.all_gather(own_rows, 'tp', axis=0, tiled=True)  48.1 us
    all_gather x1, waiting for transfers between devices, per_device(): queries = lax.all_gather(own_queries, 'tp', axis=1, tiled=True)  45.7 us
    all_to_all x1, waiting for transfers between devices, per_device(): lax.all_to_all(mixtures[None].astype(jnp.float32), 'tp', split_axis=1, co...  44.4 us
    unnamed x7, other arithmetic  22 us
    unnamed x38, local copies, waits for them, and re-layouts  13.2 us
    dot_general x4, matrix products, partial_attend(): jnp.dot(weights.astype(jnp.bfloat16).reshape(row_count * group_size, -1),...  10.1 us
  transfers between devices with their start and end apart: 8, of which 6 were waited for; matrix products, arithmetic and copies ran while one was open for 18% of the time, Pallas kernels for 0%

commit v1 on v0

--- a/solution.py
+++ b/solution.py
@@ -171,8 +171,16 @@
     peer_tops, peer_totals, peer_mix = (
         lax.all_to_all(row_tops[None], "tp", split_axis=1, concat_axis=0, tiled=True),
         lax.all_to_all(row_totals[None], "tp", split_axis=1, concat_axis=0, tiled=True),
-        lax.all_to_all(
-            mixtures[None].astype(jnp.float32), "tp", split_axis=1, concat_axis=0, tiled=True
+        jnp.concatenate(
+            lax.all_to_all(
+                jnp.stack(
+                    jnp.split(mixtures[None].astype(jnp.float32), lax.axis_size("tp"), axis=1)
+                ),
+                "tp",
+                0,
+                0,
+            ),
+            axis=0,
         ).astype(jnp.bfloat16),
     )
     own_rows = finish(peer_tops, peer_totals, peer_mix)

time: 401 us -> 374 us (0.933)
  other arithmetic: 44.4 us -> 20.4 us
  starting transfers between devices: 16.9 us -> 11.7 us
    unnamed x7 -> x3, other arithmetic: 22 us -> 1.92 us
    all_to_all x1, waiting for transfers between devices: 44.4 us -> 35.1 us  [per_device(): lax.all_to_all(jnp.stack(jnp.split(mixtures[None].astype(jnp.float32), la...]
    mul x0 -> x3, local copies, waits for them, and re-layouts: none -> 7.86 us  [the longest x2 7.76 us: finish(): parts.astype(jnp.float32).reshape(piece_count, row_count, head_count, HD)]
    all_to_all x1, waiting for transfers between devices: 0.01 us -> 5.89 us  [per_device(): lax.all_to_all(row_totals[None], 'tp', split_axis=1, concat_axis=0, tiled...]
    concatenate x4, local copies, waits for them, and re-layouts: 8.09 us -> 2.44 us  [partial_attend(): jnp.concatenate(mixtures, axis=1)]
    convert_element_type x1, other arithmetic: 6.5 us -> 1.37 us  [per_device(): mixtures[None].astype(jnp.float32)]
    all_to_all x1, waiting for transfers between devices: 0.01 us -> 4.81 us  [per_device(): lax.all_to_all(row_tops[None], 'tp', split_axis=1, concat_axis=0, tiled=T...]
    unnamed x38 -> x34, local copies, waits for them, and re-layouts: 13.2 us -> 9.48 us
  transfers between devices with their start and end apart: 8 -> 8, of which waited for: 6 -> 8; matrix products, arithmetic and copies ran while one was open for 18% -> 9% of each run, Pallas kernels for 0% -> 0%
where the time goes in v1:
time: 374 us; the launch traced here: 373 us
  waiting for transfers between devices  264 us (71%)
  matrix products  36.1 us (10%)
  local copies, waits for them, and re-layouts  26.2 us (7%)
  other arithmetic  20.4 us (5%)
  between operations  14.3 us (4%)
  starting transfers between devices  11.7 us (3%)
    all_gather x1, waiting for transfers between devices, per_device(): lax.all_gather(inputs, 'tp', axis=1, tiled=True)  69.2 us
    reduce_scatter x1, waiting for transfers between devices, per_device(): lax.psum_scatter(jnp.dot(inputs, kv_weight, preferred_element_type=jnp.fl...  54.2 us
    all_gather x1, waiting for transfers between devices, per_device(): lax.all_gather(own_rows, 'tp', axis=0, tiled=True)  48.1 us
    all_gather x1, waiting for transfers between devices, per_device(): queries = lax.all_gather(own_queries, 'tp', axis=1, tiled=True)  45.7 us
    all_to_all x1, waiting for transfers between devices, per_device(): lax.all_to_all(jnp.stack(jnp.split(mixtures[None].astype(jnp.float32), la...  35.1 us
    dot_general x4, matrix products, partial_attend(): jnp.dot(weights.astype(jnp.bfloat16).reshape(row_count * group_size, -1),...  9.8 us
    unnamed x34, local copies, waits for them, and re-layouts  9.48 us
    mul x2, local copies, waits for them, and re-layouts, finish(): parts.astype(jnp.float32).reshape(piece_count, row_count, head_count, HD)  7.76 us
  transfers between devices with their start and end apart: 8, of which 8 were waited for; matrix products, arithmetic and copies ran while one was open for 9% of the time, Pallas kernels for 0%

profile of v1, /device:TPU:0, one launch (start us, length us, event | category | flops | bytes accessed | tf_op | source)
XLA Modules:
  0.0 373.1 jit_solution(816997513177283953)
XLA Ops:
  6.5 0.7 all-gather.9.cloned.1.call-update
  7.3 0.8 copy-done
  8.1 2.5 convolution_convert_fusion.1
  10.8 1.1 convolution_minimum_fusion.5
  12.4 0.3 convolution_minimum_fusion.2
  13.0 0.4 fusion.75
  13.6 0.6 dynamic_slice.10
  14.7 0.6 fusion.72
  15.3 0.5 multiply_cosine_fusion
  15.8 69.2 %all-gather.9.cloned.1.call-done = bf16[1,1,256,8192]{3,2,1,0:T(8,128)(2,1)} async-done(((bf16[1,1,256,1024]{3,2,1,0:T(8,128)(2,1)}), bf16[1,1,256,8192]{3,2,1,0:T(8,128)(2,1)}) %all-gather.9.cloned.1.call-update) | async-done | bytes 4194320 | tf_op jit(solution)/shard_map/all_gather | solution.py:127
  85.1 7.0 %fusion = f32[256,512]{1,0:T(8,128)S(1)} fusion(bf16[8192,512]{1,0:T(8,128)(2,1)} %param.10, bf16[1,1,256,8192]{3,2,1,0:T(8,128)(2,1)} %all-gather.9.cloned.1.call-done), kind=kOutput, calls=%fused_computation.8 | convolution fusion | flops 2147483648 | bytes 13107200 | tf_op jit(solution)/shard_map/dot_general | solution.py:126
  92.2 0.5 subtract_convert_fusion
  92.7 0.4 pad_maximum_fusion.2
  93.1 0.9 copy.48
  94.3 0.3 mul.170
  94.6 0.6 fusion.54
  95.8 54.2 %reduce-scatter.2.cloned.1.call-done = bf16[32,1024]{1,0:T(8,128)(2,1)} async-done(((bf16[256,1024]{1,0:T(8,128)(2,1)}), bf16[32,1024]{1,0:T(8,128)(2,1)}) %reduce-scatter.2.cloned.1.call-update) | async-done | bytes 65552 | tf_op jit(solution)/shard_map/reduce_scatter | solution.py:137
  150.1 0.8 fusion.74
  151.1 1.3 collective-permute-start
  152.7 0.6 collective-permute-done
  153.3 1.3 pad_maximum_fusion
  154.6 45.7 %all-gather.5.cloned.1.call-done = bf16[256,4096]{0,1:T(8,128)(2,1)} async-done(((bf16[256,512]{0,1:T(8,128)(2,1)}), bf16[256,4096]{0,1:T(8,128)(2,1)}) %all-gather.5.cloned.1.call-update) | async-done | bytes 2097168 | tf_op jit(solution)/shard_map/all_gather | solution.py:136
  200.3 1.7 fusion.73
  201.9 0.8 fusion.45
  202.7 0.8 fusion.46
  203.5 0.9 fusion.2
  204.4 0.5 copy-done.2
  204.8 4.7 %fusion.6 = (f32[256,8]{0,1:T(8,128)S(1)}, f32[256,8]{0,1:T(8,128)S(1)}, f32[256,8]{0,1:T(8,128)S(1)}, f32[256,8]{0,1:T(8,128)S(1)}, f32[256,8,576]{0,2,1:T(8,128)}) fusion(f32[256,8,576]{0,2,1:T(8,128)S(1)} %get-tuple-element.36, f32[256,8]{0,1:T(8,128)S(1)} %get-tuple-element.35, pred[256,576]{0,1:T(8,128)(4,1)S(1)} %add_select_fusion, ...), kind=kOutput, calls=%fused_computation.15 | convolution fusion | flops 318496768 | bytes 19734528 | tf_op jit(solution)/shard_map/dot_general | solution.py:61
  209.5 1.3 divide_convert_fusion.3
  211.1 7.0 %fusion.8 = (f32[256,8]{0,1:T(8,128)S(1)}, f32[256,8]{0,1:T(8,128)S(1)}, f32[256,8]{0,1:T(8,128)S(1)}) fusion(f32[256,8,576]{0,2,1:T(8,128)} %get-tuple-element.37, f32[256,8]{0,1:T(8,128)S(1)} %get-tuple-element.6, pred[256,576]{0,1:T(8,128)(4,1)S(1)} %add_select_fusion, f32[256,8]{0,1:T(8,128)S(1)} %get-tuple-element.7, f32[256,8,576]{0,2,1:T(8,128)} %copy-done.3, ...), kind=kLoop, calls=%fused_computation.17 | loop fusion | flops 17688576 | bytes 14352384 | tf_op jit(solution)/shard_map/reduce_sum | solution.py:68
  218.1 1.3 divide_convert_fusion.2
  219.6 3.6 divide_convert_fusion.1
  223.2 1.0 copy.55
  224.2 3.6 divide_convert_fusion
  227.9 1.0 copy.56
  228.9 1.4 maximum_convert_fusion
  230.3 0.7 fusion.43
  231.0 0.7 fusion.42
  231.7 0.7 fusion.41
  232.4 0.7 fusion.40
  233.2 0.7 fusion.39
  233.9 0.7 fusion.38
  234.6 0.7 fusion.37
  235.5 0.5 broadcast.411
  236.0 1.0 reduce.3
  237.0 0.7 reshape.492
  237.7 3.3 all-to-all-start.1
  241.2 1.0 reduce.1
  242.1 0.7 reshape.490
  242.9 4.8 %all-to-all-done.1 = f32[8,1,1024]{2,1,0:T(1,128)S(1)} async-done(((f32[8,1,1024]{2,1,0:T(1,128)}), f32[8,1,1024]{2,1,0:T(1,128)S(1)}, u32[]{:S(2)}, u32[]{:S(2)}) %all-to-all-start.1) | async-done | bytes 32800 | tf_op jit(solution)/shard_map/all_to_all | solution.py:172
  247.7 3.3 all-to-all-start.2
  251.0 0.7 fusion.36
  251.7 5.9 %all-to-all-done.2 = f32[8,1,1024]{2,1,0:T(1,128)S(1)} async-done(((f32[8,1,1024]{2,1,0:T(1,128)}), f32[8,1,1024]{2,1,0:T(1,128)S(1)}, u32[]{:S(2)}, u32[]{:S(2)}) %all-to-all-start.2) | async-done | bytes 32800 | tf_op jit(solution)/shard_map/all_to_all | solution.py:173
  257.6 3.6 all-to-all-start
  261.3 0.7 reduce.4
  262.5 0.7 reduce.2
  263.7 2.8 mul.197
  266.5 4.9 %mul.198 = f32[8,1,32,4096]{3,2,1,0:T(8,128)} reshape(f32[8,32,32,128]{3,2,1,0:T(8,128)} %mul.197) | data formatting | bytes 8388608 | tf_op jit(solution)/shard_map/mul | solution.py:93
  271.4 35.1 %all-to-all-done = bf16[8,1,32,4096]{3,2,1,0:T(8,128)(2,1)S(1)} async-done(((bf16[8,1,32,4096]{3,2,1,0:T(8,128)(2,1)}), bf16[8,1,32,4096]{3,2,1,0:T(8,128)(2,1)S(1)}, u32[]{:S(2)}, u32[]{:S(2)}) %all-to-all-start) | async-done | bytes 2097184 | tf_op jit(solution)/shard_map/all_to_all | solution.py:175
  306.6 2.8 multiply_reduce_fusion
  309.3 0.6 copy.71
  310.1 1.0 copy.64
  311.2 48.1 %all-gather.7.cloned.1.call-done = bf16[256,4096]{1,0:T(8,128)(2,1)} async-done(((bf16[32,4096]{1,0:T(8,128)(2,1)}), bf16[256,4096]{1,0:T(8,128)(2,1)}) %all-gather.7.cloned.1.call-update) | async-done | bytes 2097168 | tf_op jit(solution)/shard_map/all_gather | solution.py:188
  359.3 7.3 %fusion.27 = bf16[1,1,256,1024]{3,2,1,0:T(8,128)(2,1)} fusion(bf16[256,4096]{1,0:T(8,128)(2,1)} %all-gather.7.cloned.1.call-done, bf16[4096,1024]{1,0:T(8,128)(2,1)} %param.12), kind=kOutput, calls=%fused_computation.36 | convolution fusion | flops 2147745792 | bytes 11010048 | tf_op jit(solution)/shard_map/dot_general | solution.py:187
  (78 shorter events, 4.5 us)
Async XLA Ops:
  6.5 1.6 copy-start
  6.5 6.9 %copy-start.6 = (s32[1,4]{1,0:T(1,128)S(1)}, s32[1,4]{1,0:T(1,128)}, u32[]{:S(2)}) copy-start(s32[1,4]{1,0:T(1,128)} %param.16) | copy-start | bytes 52
  6.5 7.0 %copy-start.7 = (s32[2]{0:T(128)S(1)}, s32[2]{0:T(128)}, u32[]{:S(2)}) copy-start(s32[2]{0:T(128)} %param.15) | copy-start | bytes 28
  6.5 78.5 %all-gather.9.cloned.1.call-start = ((), (), s32[]{:S(2)}) async-start(), calls=%async_computation.7 | async-start | bytes 4718592 | tf_op jit(solution)/shard_map/all_gather | solution.py:127
  7.3 142.8 %reduce-scatter.2.cloned.1.call-start = ((), (), s32[]{:S(2)}) async-start(), calls=%async_computation.5 | async-start | bytes 589824 | tf_op jit(solution)/shard_map/reduce_scatter | solution.py:137
  10.7 189.6 %all-gather.5.cloned.1.call-start = ((), (), s32[]{:S(2)}) async-start(), calls=%async_computation.4 | async-start | bytes 2359296 | tf_op jit(solution)/shard_map/all_gather | solution.py:136
  151.1 2.2 collective-permute-start
  154.6 54.9 %copy-start.4 = (bf16[576,512]{1,0:T(8,128)(2,1)}, bf16[576,512]{1,0:T(8,128)(2,1)S(1)}, u32[]{:S(2)}) copy-start(bf16[576,512]{1,0:T(8,128)(2,1)S(1)} %get-tuple-element.43) | copy-start | bytes 1769476
  202.7 2.1 copy-start.2
  203.5 6.0 %copy-start.3 = (f32[256,8,576]{0,2,1:T(8,128)}, f32[256,8,576]{0,2,1:T(8,128)S(1)}, u32[]{:S(2)}) copy-start(f32[256,8,576]{0,2,1:T(8,128)S(1)} %fusion.46) | copy-start | bytes 14155780
  210.8 7.2 %slice-start = ((s8[4718592]{0:T(1024)(128)(4,1)}), s8[524288]{0:T(1024)(128)(4,1)S(1)}, s32[]{:S(2)}) async-start(s8[4718592]{0:T(1024)(128)(4,1)} %bitcast.126), calls=%async_computation.8 | async-start | bytes 1048576
  211.0 7.0 %slice-start.1 = ((s8[4718592]{0:T(1024)(128)(4,1)}), s8[4194304]{0:T(1024)(128)(4,1)S(1)}, s32[]{:S(2)}) async-start(s8[4718592]{0:T(1024)(128)(4,1)} %bitcast.126), calls=%async_computation.9 | async-start | bytes 8388608
  211.1 7.0 %copy-start.5 = (bf16[576,512]{1,0:T(8,128)(2,1)S(1)}, bf16[576,512]{1,0:T(8,128)(2,1)}, u32[]{:S(2)}) copy-start(bf16[576,512]{1,0:T(8,128)(2,1)} %copy-done.4) | copy-start | bytes 1769476
  237.7 10.0 %all-to-all-start.1 = ((f32[8,1,1024]{2,1,0:T(1,128)}), f32[8,1,1024]{2,1,0:T(1,128)S(1)}, u32[]{:S(2)}, u32[]{:S(2)}) async-start(f32[8,1,1024]{2,1,0:T(1,128)} %reshape.492), calls=%async_computation.2 | async-start | bytes 65536 | tf_op jit(solution)/shard_map/all_to_all | solution.py:172
  247.7 10.0 %all-to-all-start.2 = ((f32[8,1,1024]{2,1,0:T(1,128)}), f32[8,1,1024]{2,1,0:T(1,128)S(1)}, u32[]{:S(2)}, u32[]{:S(2)}) async-start(f32[8,1,1024]{2,1,0:T(1,128)} %reshape.490), calls=%async_computation.3 | async-start | bytes 65536 | tf_op jit(solution)/shard_map/all_to_all | solution.py:173
  257.6 48.9 %all-to-all-start = ((bf16[8,1,32,4096]{3,2,1,0:T(8,128)(2,1)}), bf16[8,1,32,4096]{3,2,1,0:T(8,128)(2,1)S(1)}, u32[]{:S(2)}, u32[]{:S(2)}) async-start(bf16[8,1,32,4096]{3,2,1,0:T(8,128)(2,1)} %fusion.36), calls=%async_computation.1 | async-start | bytes 4194304 | tf_op jit(solution)/shard_map/all_to_all | solution.py:175
  261.2 98.0 %all-gather.7.cloned.1.call-start = ((), (), s32[]{:S(2)}) async-start(), calls=%async_computation.6 | async-start | bytes 2359296 | tf_op jit(solution)/shard_map/all_gather | solution.py:188
  359.3 7.3 %copy-start.1 = (bf16[1024,1024]{1,0:T(8,128)(2,1)S(1)}, bf16[1024,1024]{1,0:T(8,128)(2,1)}, u32[]{:S(2)}) copy-start(bf16[1024,1024]{1,0:T(8,128)(2,1)} %param.11) | copy-start | bytes 6291460
Sparse Core Ops, SparseCore 0:
  9.5 75.4 all-gather.8
  88.4 61.6 reduce-scatter.1
  152.2 48.0 all-gather.4
  311.3 47.9 all-gather.6
